TPU v7x, 256 devices: a whole 4x4x8 slice. The times are simulated.
256 devices in a mesh: section: 8 (over y, core), dp: 32 (over x, z).
Axes of the slice: x: 4, y: 4, z: 8, core: 2. Of those that a mesh axis runs over, the one named last changes fastest.
Arguments:
- tokens: bfloat16 [4, 1024, 2048], P(None, 'dp'), may hold values from -6 to 6
- norm_gain: bfloat16 [8, 2048], P('section'), may hold values from 0.25 to 1.75
- router_weight: bfloat16 [8, 2048, 32], P('section'), may hold values from -0.125 to 0.125
- gate_weight: bfloat16 [8, 32, 2048, 768], P('section', 'dp'), may hold values from -0.125 to 0.125
- up_weight: bfloat16 [8, 32, 2048, 768], P('section', 'dp'), may hold values from -0.125 to 0.125
- down_weight: bfloat16 [8, 32, 768, 2048], P('section', 'dp'), may hold values from -0.21875 to 0.21875
- routing: int32 [8, 4, 1024, 6], P('section', None, 'dp'), may hold values from 0 to 31, all different within a row; in each aligned block of 32 rows (0 to 31, 32 to 63, ..., all dimensions but the last counted through in order) at most 7 rows name the same one
Outputs:
- layer_outputs: bfloat16 [8, 4, 1024, 2048], P('section', None, 'dp')
- router_grad: float32 [8, 2048, 32], P('section', 'dp')
Inputs may be any that keep to these rules, and one draw needn't show every extreme that they name: `routing`: each token names 6 different experts. Among one index of dp's 32 tokens of one micro-batch and layer, at most 7 name the same expert, and in some of these blocks exactly 7 do.
All inputs are finite; a program needn't handle non-finite values.
Results may differ from a plain program's by a relative error of at most 0.019.
Values may be sent and summed in bfloat16 or wider, within the bound.
A program may use at most 64 MiB of HBM per device.

v0:
```python
import jax
import jax.numpy as jnp
from jax import lax
from jax.sharding import Mesh
from jax.sharding import PartitionSpec as P

DP = ("dp_0", "dp_1")
EPSILON = 1e-06


def over_axes(shard, axes):
    for axis in axes:
        shard = lax.psum(shard, axis)
    return shard


def from_behind(value, axis, steps):
    count = lax.axis_size(axis)
    initial, last = (max(0, -steps), min(count, count - steps))
    return lax.ppermute(value, axis, [(source, source + steps) for source in range(initial, last)])


def cut_along(shard, dim, peers):
    shape = shard.shape
    pieces = shard.reshape(*shape[:dim], peers, shape[dim] // peers, *shape[dim + 1 :])
    return jnp.moveaxis(pieces, dim, 0)


def summed_on_arrival(shard, axis, dim):
    pieces = cut_along(shard, dim, lax.axis_size(axis))
    arrived = lax.all_to_all(pieces, axis, split_axis=0, concat_axis=0, tiled=True)
    return arrived.astype(jnp.float32).sum(axis=0)


def normalize(states, gain):
    values = states.astype(jnp.float32)
    mean_square = jnp.mean(values * values, axis=-1, keepdims=True)
    return (values * lax.rsqrt(mean_square + EPSILON) * gain.astype(jnp.float32)).astype(
        jnp.bfloat16
    )


def expert_ffn(rows, w_gate, w_up, w_down):
    gated = jnp.dot(rows, w_gate, preferred_element_type=jnp.float32)
    upward = jnp.dot(rows, w_up, preferred_element_type=jnp.float32)
    hidden = (jax.nn.silu(gated) * upward).astype(jnp.bfloat16)
    return jnp.dot(hidden, w_down, preferred_element_type=jnp.float32).astype(jnp.bfloat16)


def slope_of(probs, share):
    return probs * (share - jnp.sum(probs * share, axis=-1, keepdims=True))


def outer_rows(normed_rows, slope_rows):
    return lax.dot_general(
        normed_rows.astype(jnp.float32),
        slope_rows,
        (((0,), (0,)), ((), ())),
        precision=lax.Precision.HIGHEST,
    )


def place(stack, index, value, active):
    previous = lax.dynamic_index_in_dim(stack, index, 0, keepdims=False)
    return lax.dynamic_update_index_in_dim(stack, jnp.where(active, value, previous), index, 0)


def on_device(tokens, norm_gain, router_weight, gate_weight, up_weight, down_weight, routing):
    sections = lax.axis_size("section")
    replicas = lax.axis_size(DP)
    position = lax.axis_index("section")
    micro = tokens.shape[0]
    rows = tokens.shape[1]
    width = tokens.shape[2]
    experts = router_weight.shape[2]
    chosen_count = routing.shape[3]
    slots = min(rows, rows * chosen_count // experts + 1)
    total_rows = micro * rows * replicas
    gain = norm_gain[0]
    w_router = router_weight[0]
    w_gate = gate_weight[0, 0]
    w_up = up_weight[0, 0]
    w_down = down_weight[0, 0]
    expert_ids = jnp.arange(experts, dtype=jnp.int32)
    hot_all = (routing[0][..., None] == expert_ids).astype(jnp.int32).sum(axis=2)
    local_counts = jnp.sum(hot_all, axis=(0, 1))
    slot_ids = jnp.arange(slots, dtype=jnp.int32)
    row_ids = jnp.arange(rows, dtype=jnp.int32)
    before = (row_ids[:, None] > row_ids[None, :]).astype(jnp.bfloat16)

    def section_work(states, hot, active):
        normed = normalize(states, gain)
        logits = jnp.dot(normed, w_router, preferred_element_type=jnp.float32)
        exps = jnp.exp(logits)
        probs = exps / jnp.sum(exps, axis=-1, keepdims=True)
        rank = jnp.dot(before, hot.astype(jnp.bfloat16), preferred_element_type=jnp.float32).astype(
            jnp.int32
        )
        match = ((hot.T[:, None, :] == 1) & (rank.T[:, None, :] == slot_ids[None, :, None])).astype(
            jnp.bfloat16
        )
        sent = jnp.einsum("ect,td->ecd", match, normed, preferred_element_type=jnp.float32).astype(
            jnp.bfloat16
        )

        def compute(flat):
            return expert_ffn(flat, w_gate, w_up, w_down)

        def skipped(flat):
            return jnp.zeros((flat.shape[0], width), jnp.bfloat16)

        received = lax.all_to_all(sent, DP, split_axis=0, concat_axis=0, tiled=True)
        flat = received.reshape(-1, width)
        produced = lax.cond(active, compute, skipped, flat)
        returned = lax.all_to_all(
            produced.reshape(received.shape), DP, split_axis=0, concat_axis=0, tiled=True
        )
        chosen = hot.astype(jnp.float32) * probs
        weights = (chosen / jnp.sum(chosen, axis=-1, keepdims=True)).astype(jnp.bfloat16)
        combine = match * weights.T[:, None, :]
        mixed = jnp.einsum("ect,ecd->td", combine, returned, preferred_element_type=jnp.float32)
        result = (states.astype(jnp.float32) + mixed).astype(jnp.bfloat16)
        return (result, normed, probs)

    def advance(step, incoming):
        index = step - position
        active = (index >= 0) & (index < micro)
        clipped = jnp.clip(index, 0, micro - 1)
        first = lax.dynamic_index_in_dim(tokens, jnp.minimum(step, micro - 1), 0, keepdims=False)
        states = jnp.where(position == 0, first, incoming)
        hot = lax.dynamic_index_in_dim(hot_all, clipped, 0, keepdims=False)
        result, normed, probs = section_work(states, hot, active)
        passed = from_behind(result, "section", 1)
        return (active, clipped, result, normed, probs, passed)

    steps = micro + sections - 1
    incoming = jnp.zeros((rows, width), jnp.bfloat16)
    outputs = jnp.zeros((micro, rows, width), jnp.bfloat16)
    counts = over_axes(local_counts, DP)
    share = experts * counts.astype(jnp.float32) / (chosen_count * total_rows)

    def loop_before(step, carry):
        received, stored, gradient = carry
        active, clipped, result, normed, probs, passed = advance(step, received)
        contribution = outer_rows(normed, slope_of(probs, share))
        gradient = gradient + jnp.where(active, contribution, jnp.zeros_like(contribution))
        return (passed, place(stored, clipped, result, active), gradient)

    start_carry = (incoming, outputs, jnp.zeros((width, experts), jnp.float32))
    final = lax.fori_loop(0, steps, loop_before, start_carry)
    outputs = final[1]
    grad_rows = summed_on_arrival(final[2].astype(jnp.bfloat16), DP, 0)
    return (outputs[None], grad_rows[None])


def solution(mesh):
    torus = Mesh(mesh.devices.reshape(mesh.shape["section"], 4, 8), ("section", "dp_0", "dp_1"))
    in_specs = (
        P(None, DP, None),
        P("section", None),
        P("section", None, None),
        P("section", DP, None, None),
        P("section", DP, None, None),
        P("section", DP, None, None),
        P("section", None, DP, None),
    )
    out_specs = (P("section", None, DP, None), P("section", DP, None))
    return jax.shard_map(
        on_device, mesh=torus, in_specs=in_specs, out_specs=out_specs, check_vma=False
    )
```

profile of v0, /device:TPU:8, one launch (start us, length us, event | category | flops | bytes accessed | tf_op | source)
XLA Modules:
  0.0 916.3 jit_solution(12094145917065917706)
XLA Ops:
  1.5 8.9 psum.14
  10.4 16.1 %psum.15 = s32[32]{0:T(128)S(1)} all-reduce(s32[32]{0:T(128)S(1)} %psum.14), channel_id=1, replica_groups=mesh['section'=8,'dp_0'=4,'dp_1'=8] {'dp_1'}, use_global_device_ids=true, to_apply=%region_3.0 | all-reduce | flops 32 | bytes 256 | tf_op jit(solution)/shard_map/psum | solution.py:13
  29.3 867.1 %while.19 = (s32[]{:T(128)}, bf16[32,2048]{1,0:T(8,128)(2,1)S(1)}, bf16[4,32,2048]{2,1,0:T(8,128)(2,1)}, f32[2048,32]{0,1:T(8,128)S(1)}, pred[]{:T(512)}, /*inde...) while((s32[]{:T(128)}, bf16[32,2048]{1,0:T(8,128)(2,1)S(1)}, ...), condition=%wide.region_11.12_spmd.clone, body=%wide.region_4.11_spmd.clone.sunk | while | flops 2205590528 | bytes 29810108 | solution.py:150
  37.0 23.3 %all-to-all-done = bf16[32,7,2048]{2,1,0:T(8,128)(2,1)S(1)} async-done(((bf16[32,7,2048]{2,1,0:T(8,128)(2,1)}), bf16[32,7,2048]{2,1,0:T(8,128)(2,1)S(1)}, u32[]{:S(2)}, u32[]{:S(2)}) %all-to-all-start) | async-done | bytes 917536 | tf_op jit(solution)/shard_map/while/body/eval_jaxpr/all_to_all | solution.py:112
  68.7 21.5 %all-to-all-done.1 = bf16[32,7,2048]{2,1,0:T(8,128)(2,1)S(1)} async-done(((bf16[32,7,2048]{2,1,0:T(8,128)(2,1)}), bf16[32,7,2048]{2,1,0:T(8,128)(2,1)S(1)}, u32[]{:S(2)}, u32[]{:S(2)}) %all-to-all-start.1) | async-done | bytes 917536 | tf_op jit(solution)/shard_map/while/body/eval_jaxpr/all_to_all | solution.py:115
  107.0 28.2 %all-to-all-done = bf16[32,7,2048]{2,1,0:T(8,128)(2,1)S(1)} async-done(((bf16[32,7,2048]{2,1,0:T(8,128)(2,1)}), bf16[32,7,2048]{2,1,0:T(8,128)(2,1)S(1)}, u32[]{:S(2)}, u32[]{:S(2)}) %all-to-all-start) | async-done | bytes 917536 | tf_op jit(solution)/shard_map/while/body/eval_jaxpr/all_to_all | solution.py:112
  143.0 26.8 %all-to-all-done.1 = bf16[32,7,2048]{2,1,0:T(8,128)(2,1)S(1)} async-done(((bf16[32,7,2048]{2,1,0:T(8,128)(2,1)}), bf16[32,7,2048]{2,1,0:T(8,128)(2,1)S(1)}, u32[]{:S(2)}, u32[]{:S(2)}) %all-to-all-start.1) | async-done | bytes 917536 | tf_op jit(solution)/shard_map/while/body/eval_jaxpr/all_to_all | solution.py:115
  185.0 8.7 all-to-all-start
  193.8 20.4 %all-to-all-done = bf16[32,7,2048]{2,1,0:T(8,128)(2,1)S(1)} async-done(((bf16[32,7,2048]{2,1,0:T(8,128)(2,1)}), bf16[32,7,2048]{2,1,0:T(8,128)(2,1)S(1)}, u32[]{:S(2)}, u32[]{:S(2)}) %all-to-all-start) | async-done | bytes 917536 | tf_op jit(solution)/shard_map/while/body/eval_jaxpr/all_to_all | solution.py:112
  214.2 8.9 conditional.3
  230.2 16.7 %all-to-all-done.1 = bf16[32,7,2048]{2,1,0:T(8,128)(2,1)S(1)} async-done(((bf16[32,7,2048]{2,1,0:T(8,128)(2,1)}), bf16[32,7,2048]{2,1,0:T(8,128)(2,1)S(1)}, u32[]{:S(2)}, u32[]{:S(2)}) %all-to-all-start.1) | async-done | bytes 917536 | tf_op jit(solution)/shard_map/while/body/eval_jaxpr/all_to_all | solution.py:115
  250.5 17.6 %collective-permute-done = bf16[32,2048]{1,0:T(8,128)(2,1)S(1)} collective-permute-done((bf16[32,2048]{1,0:T(8,128)(2,1)S(1)}, bf16[32,2048]{1,0:T(8,128)(2,1)S(1)}, u32[]{:S(2)}, u32[]{:S(2)}) %collective-permute-start) | collective-permute-done | bytes 131104 | tf_op jit(solution)/shard_map/while/body/eval_jaxpr/ppermute | solution.py:20
  271.6 8.3 all-to-all-start
  279.9 18.1 %all-to-all-done = bf16[32,7,2048]{2,1,0:T(8,128)(2,1)S(1)} async-done(((bf16[32,7,2048]{2,1,0:T(8,128)(2,1)}), bf16[32,7,2048]{2,1,0:T(8,128)(2,1)S(1)}, u32[]{:S(2)}, u32[]{:S(2)}) %all-to-all-start) | async-done | bytes 917536 | tf_op jit(solution)/shard_map/while/body/eval_jaxpr/all_to_all | solution.py:112
  298.0 8.9 conditional.3
  315.9 16.7 %all-to-all-done.1 = bf16[32,7,2048]{2,1,0:T(8,128)(2,1)S(1)} async-done(((bf16[32,7,2048]{2,1,0:T(8,128)(2,1)}), bf16[32,7,2048]{2,1,0:T(8,128)(2,1)S(1)}, u32[]{:S(2)}, u32[]{:S(2)}) %all-to-all-start.1) | async-done | bytes 917536 | tf_op jit(solution)/shard_map/while/body/eval_jaxpr/all_to_all | solution.py:115
  336.2 18.0 %collective-permute-done = bf16[32,2048]{1,0:T(8,128)(2,1)S(1)} collective-permute-done((bf16[32,2048]{1,0:T(8,128)(2,1)S(1)}, bf16[32,2048]{1,0:T(8,128)(2,1)S(1)}, u32[]{:S(2)}, u32[]{:S(2)}) %collective-permute-start) | collective-permute-done | bytes 131104 | tf_op jit(solution)/shard_map/while/body/eval_jaxpr/ppermute | solution.py:20
  365.9 18.1 %all-to-all-done = bf16[32,7,2048]{2,1,0:T(8,128)(2,1)S(1)} async-done(((bf16[32,7,2048]{2,1,0:T(8,128)(2,1)}), bf16[32,7,2048]{2,1,0:T(8,128)(2,1)S(1)}, u32[]{:S(2)}, u32[]{:S(2)}) %all-to-all-start) | async-done | bytes 917536 | tf_op jit(solution)/shard_map/while/body/eval_jaxpr/all_to_all | solution.py:112
  384.0 8.9 conditional.3
  402.0 16.7 %all-to-all-done.1 = bf16[32,7,2048]{2,1,0:T(8,128)(2,1)S(1)} async-done(((bf16[32,7,2048]{2,1,0:T(8,128)(2,1)}), bf16[32,7,2048]{2,1,0:T(8,128)(2,1)S(1)}, u32[]{:S(2)}, u32[]{:S(2)}) %all-to-all-start.1) | async-done | bytes 917536 | tf_op jit(solution)/shard_map/while/body/eval_jaxpr/all_to_all | solution.py:115
  422.3 13.1 %collective-permute-done = bf16[32,2048]{1,0:T(8,128)(2,1)S(1)} collective-permute-done((bf16[32,2048]{1,0:T(8,128)(2,1)S(1)}, bf16[32,2048]{1,0:T(8,128)(2,1)S(1)}, u32[]{:S(2)}, u32[]{:S(2)}) %collective-permute-start) | collective-permute-done | bytes 131104 | tf_op jit(solution)/shard_map/while/body/eval_jaxpr/ppermute | solution.py:20
  444.8 17.4 %all-to-all-done = bf16[32,7,2048]{2,1,0:T(8,128)(2,1)S(1)} async-done(((bf16[32,7,2048]{2,1,0:T(8,128)(2,1)}), bf16[32,7,2048]{2,1,0:T(8,128)(2,1)S(1)}, u32[]{:S(2)}, u32[]{:S(2)}) %all-to-all-start) | async-done | bytes 917536 | tf_op jit(solution)/shard_map/while/body/eval_jaxpr/all_to_all | solution.py:112
  462.3 8.9 conditional.3
  480.4 16.7 %all-to-all-done.1 = bf16[32,7,2048]{2,1,0:T(8,128)(2,1)S(1)} async-done(((bf16[32,7,2048]{2,1,0:T(8,128)(2,1)}), bf16[32,7,2048]{2,1,0:T(8,128)(2,1)S(1)}, u32[]{:S(2)}, u32[]{:S(2)}) %all-to-all-start.1) | async-done | bytes 917536 | tf_op jit(solution)/shard_map/while/body/eval_jaxpr/all_to_all | solution.py:115
  500.7 9.6 %collective-permute-done = bf16[32,2048]{1,0:T(8,128)(2,1)S(1)} collective-permute-done((bf16[32,2048]{1,0:T(8,128)(2,1)S(1)}, bf16[32,2048]{1,0:T(8,128)(2,1)S(1)}, u32[]{:S(2)}, u32[]{:S(2)}) %collective-permute-start) | collective-permute-done | bytes 131104 | tf_op jit(solution)/shard_map/while/body/eval_jaxpr/ppermute | solution.py:20
  522.1 17.8 %all-to-all-done = bf16[32,7,2048]{2,1,0:T(8,128)(2,1)S(1)} async-done(((bf16[32,7,2048]{2,1,0:T(8,128)(2,1)}), bf16[32,7,2048]{2,1,0:T(8,128)(2,1)S(1)}, u32[]{:S(2)}, u32[]{:S(2)}) %all-to-all-start) | async-done | bytes 917536 | tf_op jit(solution)/shard_map/while/body/eval_jaxpr/all_to_all | solution.py:112
  548.8 24.1 %all-to-all-done.1 = bf16[32,7,2048]{2,1,0:T(8,128)(2,1)S(1)} async-done(((bf16[32,7,2048]{2,1,0:T(8,128)(2,1)}), bf16[32,7,2048]{2,1,0:T(8,128)(2,1)S(1)}, u32[]{:S(2)}, u32[]{:S(2)}) %all-to-all-start.1) | async-done | bytes 917536 | tf_op jit(solution)/shard_map/while/body/eval_jaxpr/all_to_all | solution.py:115
  576.6 10.9 %collective-permute-done = bf16[32,2048]{1,0:T(8,128)(2,1)S(1)} collective-permute-done((bf16[32,2048]{1,0:T(8,128)(2,1)S(1)}, bf16[32,2048]{1,0:T(8,128)(2,1)S(1)}, u32[]{:S(2)}, u32[]{:S(2)}) %collective-permute-start) | collective-permute-done | bytes 131104 | tf_op jit(solution)/shard_map/while/body/eval_jaxpr/ppermute | solution.py:20
  591.0 8.3 all-to-all-start
  599.3 18.1 %all-to-all-done = bf16[32,7,2048]{2,1,0:T(8,128)(2,1)S(1)} async-done(((bf16[32,7,2048]{2,1,0:T(8,128)(2,1)}), bf16[32,7,2048]{2,1,0:T(8,128)(2,1)S(1)}, u32[]{:S(2)}, u32[]{:S(2)}) %all-to-all-start) | async-done | bytes 917536 | tf_op jit(solution)/shard_map/while/body/eval_jaxpr/all_to_all | solution.py:112
  618.8 8.4 all-to-all-start.1
  628.7 16.7 %all-to-all-done.1 = bf16[32,7,2048]{2,1,0:T(8,128)(2,1)S(1)} async-done(((bf16[32,7,2048]{2,1,0:T(8,128)(2,1)}), bf16[32,7,2048]{2,1,0:T(8,128)(2,1)S(1)}, u32[]{:S(2)}, u32[]{:S(2)}) %all-to-all-start.1) | async-done | bytes 917536 | tf_op jit(solution)/shard_map/while/body/eval_jaxpr/all_to_all | solution.py:115
  649.0 15.8 %collective-permute-done = bf16[32,2048]{1,0:T(8,128)(2,1)S(1)} collective-permute-done((bf16[32,2048]{1,0:T(8,128)(2,1)S(1)}, bf16[32,2048]{1,0:T(8,128)(2,1)S(1)}, u32[]{:S(2)}, u32[]{:S(2)}) %collective-permute-start) | collective-permute-done | bytes 131104 | tf_op jit(solution)/shard_map/while/body/eval_jaxpr/ppermute | solution.py:20
  668.2 8.3 all-to-all-start
  676.5 20.5 %all-to-all-done = bf16[32,7,2048]{2,1,0:T(8,128)(2,1)S(1)} async-done(((bf16[32,7,2048]{2,1,0:T(8,128)(2,1)}), bf16[32,7,2048]{2,1,0:T(8,128)(2,1)S(1)}, u32[]{:S(2)}, u32[]{:S(2)}) %all-to-all-start) | async-done | bytes 917536 | tf_op jit(solution)/shard_map/while/body/eval_jaxpr/all_to_all | solution.py:112
  698.4 10.2 %all-to-all-start.1 = ((bf16[32,7,2048]{2,1,0:T(8,128)(2,1)}), bf16[32,7,2048]{2,1,0:T(8,128)(2,1)S(1)}, u32[]{:S(2)}, u32[]{:S(2)}) async-start(bf16[32,7,2048]{2,1,0:T(8,128)(2,1)} %reshape.63), calls=%async_computation.1 | async-start | bytes 2097152 | tf_op jit(solution)/shard_map/while/body/eval_jaxpr/all_to_all | solution.py:115
  710.1 16.7 %all-to-all-done.1 = bf16[32,7,2048]{2,1,0:T(8,128)(2,1)S(1)} async-done(((bf16[32,7,2048]{2,1,0:T(8,128)(2,1)}), bf16[32,7,2048]{2,1,0:T(8,128)(2,1)S(1)}, u32[]{:S(2)}, u32[]{:S(2)}) %all-to-all-start.1) | async-done | bytes 917536 | tf_op jit(solution)/shard_map/while/body/eval_jaxpr/all_to_all | solution.py:115
  730.4 11.6 %collective-permute-done = bf16[32,2048]{1,0:T(8,128)(2,1)S(1)} collective-permute-done((bf16[32,2048]{1,0:T(8,128)(2,1)S(1)}, bf16[32,2048]{1,0:T(8,128)(2,1)S(1)}, u32[]{:S(2)}, u32[]{:S(2)}) %collective-permute-start) | collective-permute-done | bytes 131104 | tf_op jit(solution)/shard_map/while/body/eval_jaxpr/ppermute | solution.py:20
  745.4 8.3 all-to-all-start
  753.7 18.1 %all-to-all-done = bf16[32,7,2048]{2,1,0:T(8,128)(2,1)S(1)} async-done(((bf16[32,7,2048]{2,1,0:T(8,128)(2,1)}), bf16[32,7,2048]{2,1,0:T(8,128)(2,1)S(1)}, u32[]{:S(2)}, u32[]{:S(2)}) %all-to-all-start) | async-done | bytes 917536 | tf_op jit(solution)/shard_map/while/body/eval_jaxpr/all_to_all | solution.py:112
  782.9 16.7 %all-to-all-done.1 = bf16[32,7,2048]{2,1,0:T(8,128)(2,1)S(1)} async-done(((bf16[32,7,2048]{2,1,0:T(8,128)(2,1)}), bf16[32,7,2048]{2,1,0:T(8,128)(2,1)S(1)}, u32[]{:S(2)}, u32[]{:S(2)}) %all-to-all-start.1) | async-done | bytes 917536 | tf_op jit(solution)/shard_map/while/body/eval_jaxpr/all_to_all | solution.py:115
  803.2 16.0 %collective-permute-done = bf16[32,2048]{1,0:T(8,128)(2,1)S(1)} collective-permute-done((bf16[32,2048]{1,0:T(8,128)(2,1)S(1)}, bf16[32,2048]{1,0:T(8,128)(2,1)S(1)}, u32[]{:S(2)}, u32[]{:S(2)}) %collective-permute-start) | collective-permute-done | bytes 131104 | tf_op jit(solution)/shard_map/while/body/eval_jaxpr/ppermute | solution.py:20
  822.7 8.3 all-to-all-start
  831.0 20.9 %all-to-all-done = bf16[32,7,2048]{2,1,0:T(8,128)(2,1)S(1)} async-done(((bf16[32,7,2048]{2,1,0:T(8,128)(2,1)}), bf16[32,7,2048]{2,1,0:T(8,128)(2,1)S(1)}, u32[]{:S(2)}, u32[]{:S(2)}) %all-to-all-start) | async-done | bytes 917536 | tf_op jit(solution)/shard_map/while/body/eval_jaxpr/all_to_all | solution.py:112
  853.3 9.8 %all-to-all-start.1 = ((bf16[32,7,2048]{2,1,0:T(8,128)(2,1)}), bf16[32,7,2048]{2,1,0:T(8,128)(2,1)S(1)}, u32[]{:S(2)}, u32[]{:S(2)}) async-start(bf16[32,7,2048]{2,1,0:T(8,128)(2,1)} %reshape.63), calls=%async_computation.1 | async-start | bytes 2097152 | tf_op jit(solution)/shard_map/while/body/eval_jaxpr/all_to_all | solution.py:115
  864.6 16.7 %all-to-all-done.1 = bf16[32,7,2048]{2,1,0:T(8,128)(2,1)S(1)} async-done(((bf16[32,7,2048]{2,1,0:T(8,128)(2,1)}), bf16[32,7,2048]{2,1,0:T(8,128)(2,1)S(1)}, u32[]{:S(2)}, u32[]{:S(2)}) %all-to-all-start.1) | async-done | bytes 917536 | tf_op jit(solution)/shard_map/while/body/eval_jaxpr/all_to_all | solution.py:115
  884.9 11.6 %collective-permute-done = bf16[32,2048]{1,0:T(8,128)(2,1)S(1)} collective-permute-done((bf16[32,2048]{1,0:T(8,128)(2,1)S(1)}, bf16[32,2048]{1,0:T(8,128)(2,1)S(1)}, u32[]{:S(2)}, u32[]{:S(2)}) %collective-permute-start) | collective-permute-done | bytes 131104 | tf_op jit(solution)/shard_map/while/body/eval_jaxpr/ppermute | solution.py:20
  897.0 18.4 %all_to_all.29 = bf16[32,2,1024]{2,1,0:T(2,128)(2,1)S(1)} all-to-all(bf16[32,2,1024]{2,1,0:T(2,128)(2,1)S(1)} %reshape.60), channel_id=1, replica_groups=mesh['section'=8,'dp_0'=4,'dp_1'=8] {'dp_0','dp_1'}, dimensions={0} | all-to-all | bytes 262144 | tf_op jit(solution)/shard_map/all_to_all | solution.py:31
  (275 shorter events, 242.1 us)
Async XLA Ops:
  32.8 27.5 %all-to-all-start = ((bf16[32,7,2048]{2,1,0:T(8,128)(2,1)}), bf16[32,7,2048]{2,1,0:T(8,128)(2,1)S(1)}, u32[]{:S(2)}, u32[]{:S(2)}) async-start(bf16[32,7,2048]{2,1,0:T(8,128)(2,1)} %copy.69), calls=%async_computation | async-start | bytes 2097152 | tf_op jit(solution)/shard_map/while/body/eval_jaxpr/all_to_all | solution.py:112
  61.7 28.5 %all-to-all-start.1 = ((bf16[32,7,2048]{2,1,0:T(8,128)(2,1)}), bf16[32,7,2048]{2,1,0:T(8,128)(2,1)S(1)}, u32[]{:S(2)}, u32[]{:S(2)}) async-start(bf16[32,7,2048]{2,1,0:T(8,128)(2,1)} %reshape.63), calls=%async_computation.1 | async-start | bytes 2097152 | tf_op jit(solution)/shard_map/while/body/eval_jaxpr/all_to_all | solution.py:115
  91.6 6.3 collective-permute-start
  101.3 33.9 %all-to-all-start = ((bf16[32,7,2048]{2,1,0:T(8,128)(2,1)}), bf16[32,7,2048]{2,1,0:T(8,128)(2,1)S(1)}, u32[]{:S(2)}, u32[]{:S(2)}) async-start(bf16[32,7,2048]{2,1,0:T(8,128)(2,1)} %copy.69), calls=%async_computation | async-start | bytes 2097152 | tf_op jit(solution)/shard_map/while/body/eval_jaxpr/all_to_all | solution.py:112
  136.6 33.2 %all-to-all-start.1 = ((bf16[32,7,2048]{2,1,0:T(8,128)(2,1)}), bf16[32,7,2048]{2,1,0:T(8,128)(2,1)S(1)}, u32[]{:S(2)}, u32[]{:S(2)}) async-start(bf16[32,7,2048]{2,1,0:T(8,128)(2,1)} %reshape.63), calls=%async_computation.1 | async-start | bytes 2097152 | tf_op jit(solution)/shard_map/while/body/eval_jaxpr/all_to_all | solution.py:115
  171.2 10.3 %collective-permute-start = (bf16[32,2048]{1,0:T(8,128)(2,1)S(1)}, bf16[32,2048]{1,0:T(8,128)(2,1)S(1)}, u32[]{:S(2)}, u32[]{:S(2)}) collective-permute-start(bf16[32,2048]{1,0:T(8,128)(2,1)S(1)} %get-tuple-element.542), channel_id=1, source_target_pairs={{0,32},{32,64},{64,96},{96,128},{128,160},{160,192},{192,224},{1,3... | collective-permute-start | bytes 393224 | tf_op jit(solution)/shard_map/while/body/eval_jaxpr/ppermute | solution.py:20
  185.0 29.2 %all-to-all-start = ((bf16[32,7,2048]{2,1,0:T(8,128)(2,1)}), bf16[32,7,2048]{2,1,0:T(8,128)(2,1)S(1)}, u32[]{:S(2)}, u32[]{:S(2)}) async-start(bf16[32,7,2048]{2,1,0:T(8,128)(2,1)} %copy.69), calls=%async_computation | async-start | bytes 2097152 | tf_op jit(solution)/shard_map/while/body/eval_jaxpr/all_to_all | solution.py:112
  224.4 22.4 %all-to-all-start.1 = ((bf16[32,7,2048]{2,1,0:T(8,128)(2,1)}), bf16[32,7,2048]{2,1,0:T(8,128)(2,1)S(1)}, u32[]{:S(2)}, u32[]{:S(2)}) async-start(bf16[32,7,2048]{2,1,0:T(8,128)(2,1)} %reshape.63), calls=%async_computation.1 | async-start | bytes 2097152 | tf_op jit(solution)/shard_map/while/body/eval_jaxpr/all_to_all | solution.py:115
  248.2 19.9 %collective-permute-start = (bf16[32,2048]{1,0:T(8,128)(2,1)S(1)}, bf16[32,2048]{1,0:T(8,128)(2,1)S(1)}, u32[]{:S(2)}, u32[]{:S(2)}) collective-permute-start(bf16[32,2048]{1,0:T(8,128)(2,1)S(1)} %get-tuple-element.542), channel_id=1, source_target_pairs={{0,32},{32,64},{64,96},{96,128},{128,160},{160,192},{192,224},{1,3... | collective-permute-start | bytes 393224 | tf_op jit(solution)/shard_map/while/body/eval_jaxpr/ppermute | solution.py:20
  271.6 26.4 %all-to-all-start = ((bf16[32,7,2048]{2,1,0:T(8,128)(2,1)}), bf16[32,7,2048]{2,1,0:T(8,128)(2,1)S(1)}, u32[]{:S(2)}, u32[]{:S(2)}) async-start(bf16[32,7,2048]{2,1,0:T(8,128)(2,1)} %copy.69), calls=%async_computation | async-start | bytes 2097152 | tf_op jit(solution)/shard_map/while/body/eval_jaxpr/all_to_all | solution.py:112
  308.2 24.4 %all-to-all-start.1 = ((bf16[32,7,2048]{2,1,0:T(8,128)(2,1)}), bf16[32,7,2048]{2,1,0:T(8,128)(2,1)S(1)}, u32[]{:S(2)}, u32[]{:S(2)}) async-start(bf16[32,7,2048]{2,1,0:T(8,128)(2,1)} %reshape.63), calls=%async_computation.1 | async-start | bytes 2097152 | tf_op jit(solution)/shard_map/while/body/eval_jaxpr/all_to_all | solution.py:115
  334.0 20.2 %collective-permute-start = (bf16[32,2048]{1,0:T(8,128)(2,1)S(1)}, bf16[32,2048]{1,0:T(8,128)(2,1)S(1)}, u32[]{:S(2)}, u32[]{:S(2)}) collective-permute-start(bf16[32,2048]{1,0:T(8,128)(2,1)S(1)} %get-tuple-element.542), channel_id=1, source_target_pairs={{0,32},{32,64},{64,96},{96,128},{128,160},{160,192},{192,224},{1,3... | collective-permute-start | bytes 393224 | tf_op jit(solution)/shard_map/while/body/eval_jaxpr/ppermute | solution.py:20
  357.6 26.4 %all-to-all-start = ((bf16[32,7,2048]{2,1,0:T(8,128)(2,1)}), bf16[32,7,2048]{2,1,0:T(8,128)(2,1)S(1)}, u32[]{:S(2)}, u32[]{:S(2)}) async-start(bf16[32,7,2048]{2,1,0:T(8,128)(2,1)} %copy.69), calls=%async_computation | async-start | bytes 2097152 | tf_op jit(solution)/shard_map/while/body/eval_jaxpr/all_to_all | solution.py:112
  394.3 24.4 %all-to-all-start.1 = ((bf16[32,7,2048]{2,1,0:T(8,128)(2,1)}), bf16[32,7,2048]{2,1,0:T(8,128)(2,1)S(1)}, u32[]{:S(2)}, u32[]{:S(2)}) async-start(bf16[32,7,2048]{2,1,0:T(8,128)(2,1)} %reshape.63), calls=%async_computation.1 | async-start | bytes 2097152 | tf_op jit(solution)/shard_map/while/body/eval_jaxpr/all_to_all | solution.py:115
  420.0 15.4 %collective-permute-start = (bf16[32,2048]{1,0:T(8,128)(2,1)S(1)}, bf16[32,2048]{1,0:T(8,128)(2,1)S(1)}, u32[]{:S(2)}, u32[]{:S(2)}) collective-permute-start(bf16[32,2048]{1,0:T(8,128)(2,1)S(1)} %get-tuple-element.542), channel_id=1, source_target_pairs={{0,32},{32,64},{64,96},{96,128},{128,160},{160,192},{192,224},{1,3... | collective-permute-start | bytes 393224 | tf_op jit(solution)/shard_map/while/body/eval_jaxpr/ppermute | solution.py:20
  438.9 23.4 %all-to-all-start = ((bf16[32,7,2048]{2,1,0:T(8,128)(2,1)}), bf16[32,7,2048]{2,1,0:T(8,128)(2,1)S(1)}, u32[]{:S(2)}, u32[]{:S(2)}) async-start(bf16[32,7,2048]{2,1,0:T(8,128)(2,1)} %copy.69), calls=%async_computation | async-start | bytes 2097152 | tf_op jit(solution)/shard_map/while/body/eval_jaxpr/all_to_all | solution.py:112
  472.5 24.6 %all-to-all-start.1 = ((bf16[32,7,2048]{2,1,0:T(8,128)(2,1)}), bf16[32,7,2048]{2,1,0:T(8,128)(2,1)S(1)}, u32[]{:S(2)}, u32[]{:S(2)}) async-start(bf16[32,7,2048]{2,1,0:T(8,128)(2,1)} %reshape.63), calls=%async_computation.1 | async-start | bytes 2097152 | tf_op jit(solution)/shard_map/while/body/eval_jaxpr/all_to_all | solution.py:115
  498.5 11.8 %collective-permute-start = (bf16[32,2048]{1,0:T(8,128)(2,1)S(1)}, bf16[32,2048]{1,0:T(8,128)(2,1)S(1)}, u32[]{:S(2)}, u32[]{:S(2)}) collective-permute-start(bf16[32,2048]{1,0:T(8,128)(2,1)S(1)} %get-tuple-element.542), channel_id=1, source_target_pairs={{0,32},{32,64},{64,96},{96,128},{128,160},{160,192},{192,224},{1,3... | collective-permute-start | bytes 393224 | tf_op jit(solution)/shard_map/while/body/eval_jaxpr/ppermute | solution.py:20
  513.8 26.1 %all-to-all-start = ((bf16[32,7,2048]{2,1,0:T(8,128)(2,1)}), bf16[32,7,2048]{2,1,0:T(8,128)(2,1)S(1)}, u32[]{:S(2)}, u32[]{:S(2)}) async-start(bf16[32,7,2048]{2,1,0:T(8,128)(2,1)} %copy.69), calls=%async_computation | async-start | bytes 2097152 | tf_op jit(solution)/shard_map/while/body/eval_jaxpr/all_to_all | solution.py:112
  541.3 31.7 %all-to-all-start.1 = ((bf16[32,7,2048]{2,1,0:T(8,128)(2,1)}), bf16[32,7,2048]{2,1,0:T(8,128)(2,1)S(1)}, u32[]{:S(2)}, u32[]{:S(2)}) async-start(bf16[32,7,2048]{2,1,0:T(8,128)(2,1)} %reshape.63), calls=%async_computation.1 | async-start | bytes 2097152 | tf_op jit(solution)/shard_map/while/body/eval_jaxpr/all_to_all | solution.py:115
  574.4 13.2 %collective-permute-start = (bf16[32,2048]{1,0:T(8,128)(2,1)S(1)}, bf16[32,2048]{1,0:T(8,128)(2,1)S(1)}, u32[]{:S(2)}, u32[]{:S(2)}) collective-permute-start(bf16[32,2048]{1,0:T(8,128)(2,1)S(1)} %get-tuple-element.542), channel_id=1, source_target_pairs={{0,32},{32,64},{64,96},{96,128},{128,160},{160,192},{192,224},{1,3... | collective-permute-start | bytes 393224 | tf_op jit(solution)/shard_map/while/body/eval_jaxpr/ppermute | solution.py:20
  591.0 26.4 %all-to-all-start = ((bf16[32,7,2048]{2,1,0:T(8,128)(2,1)}), bf16[32,7,2048]{2,1,0:T(8,128)(2,1)S(1)}, u32[]{:S(2)}, u32[]{:S(2)}) async-start(bf16[32,7,2048]{2,1,0:T(8,128)(2,1)} %copy.69), calls=%async_computation | async-start | bytes 2097152 | tf_op jit(solution)/shard_map/while/body/eval_jaxpr/all_to_all | solution.py:112
  618.8 26.5 %all-to-all-start.1 = ((bf16[32,7,2048]{2,1,0:T(8,128)(2,1)}), bf16[32,7,2048]{2,1,0:T(8,128)(2,1)S(1)}, u32[]{:S(2)}, u32[]{:S(2)}) async-start(bf16[32,7,2048]{2,1,0:T(8,128)(2,1)} %reshape.63), calls=%async_computation.1 | async-start | bytes 2097152 | tf_op jit(solution)/shard_map/while/body/eval_jaxpr/all_to_all | solution.py:115
  646.7 18.0 %collective-permute-start = (bf16[32,2048]{1,0:T(8,128)(2,1)S(1)}, bf16[32,2048]{1,0:T(8,128)(2,1)S(1)}, u32[]{:S(2)}, u32[]{:S(2)}) collective-permute-start(bf16[32,2048]{1,0:T(8,128)(2,1)S(1)} %get-tuple-element.542), channel_id=1, source_target_pairs={{0,32},{32,64},{64,96},{96,128},{128,160},{160,192},{192,224},{1,3... | collective-permute-start | bytes 393224 | tf_op jit(solution)/shard_map/while/body/eval_jaxpr/ppermute | solution.py:20
  668.2 28.8 %all-to-all-start = ((bf16[32,7,2048]{2,1,0:T(8,128)(2,1)}), bf16[32,7,2048]{2,1,0:T(8,128)(2,1)S(1)}, u32[]{:S(2)}, u32[]{:S(2)}) async-start(bf16[32,7,2048]{2,1,0:T(8,128)(2,1)} %copy.69), calls=%async_computation | async-start | bytes 2097152 | tf_op jit(solution)/shard_map/while/body/eval_jaxpr/all_to_all | solution.py:112
  698.4 28.3 %all-to-all-start.1 = ((bf16[32,7,2048]{2,1,0:T(8,128)(2,1)}), bf16[32,7,2048]{2,1,0:T(8,128)(2,1)S(1)}, u32[]{:S(2)}, u32[]{:S(2)}) async-start(bf16[32,7,2048]{2,1,0:T(8,128)(2,1)} %reshape.63), calls=%async_computation.1 | async-start | bytes 2097152 | tf_op jit(solution)/shard_map/while/body/eval_jaxpr/all_to_all | solution.py:115
  728.2 13.8 %collective-permute-start = (bf16[32,2048]{1,0:T(8,128)(2,1)S(1)}, bf16[32,2048]{1,0:T(8,128)(2,1)S(1)}, u32[]{:S(2)}, u32[]{:S(2)}) collective-permute-start(bf16[32,2048]{1,0:T(8,128)(2,1)S(1)} %get-tuple-element.542), channel_id=1, source_target_pairs={{0,32},{32,64},{64,96},{96,128},{128,160},{160,192},{192,224},{1,3... | collective-permute-start | bytes 393224 | tf_op jit(solution)/shard_map/while/body/eval_jaxpr/ppermute | solution.py:20
  745.4 26.4 %all-to-all-start = ((bf16[32,7,2048]{2,1,0:T(8,128)(2,1)}), bf16[32,7,2048]{2,1,0:T(8,128)(2,1)S(1)}, u32[]{:S(2)}, u32[]{:S(2)}) async-start(bf16[32,7,2048]{2,1,0:T(8,128)(2,1)} %copy.69), calls=%async_computation | async-start | bytes 2097152 | tf_op jit(solution)/shard_map/while/body/eval_jaxpr/all_to_all | solution.py:112
  773.2 26.3 %all-to-all-start.1 = ((bf16[32,7,2048]{2,1,0:T(8,128)(2,1)}), bf16[32,7,2048]{2,1,0:T(8,128)(2,1)S(1)}, u32[]{:S(2)}, u32[]{:S(2)}) async-start(bf16[32,7,2048]{2,1,0:T(8,128)(2,1)} %reshape.63), calls=%async_computation.1 | async-start | bytes 2097152 | tf_op jit(solution)/shard_map/while/body/eval_jaxpr/all_to_all | solution.py:115
  801.0 18.2 %collective-permute-start = (bf16[32,2048]{1,0:T(8,128)(2,1)S(1)}, bf16[32,2048]{1,0:T(8,128)(2,1)S(1)}, u32[]{:S(2)}, u32[]{:S(2)}) collective-permute-start(bf16[32,2048]{1,0:T(8,128)(2,1)S(1)} %get-tuple-element.542), channel_id=1, source_target_pairs={{0,32},{32,64},{64,96},{96,128},{128,160},{160,192},{192,224},{1,3... | collective-permute-start | bytes 393224 | tf_op jit(solution)/shard_map/while/body/eval_jaxpr/ppermute | solution.py:20
  822.7 29.2 %all-to-all-start = ((bf16[32,7,2048]{2,1,0:T(8,128)(2,1)}), bf16[32,7,2048]{2,1,0:T(8,128)(2,1)S(1)}, u32[]{:S(2)}, u32[]{:S(2)}) async-start(bf16[32,7,2048]{2,1,0:T(8,128)(2,1)} %copy.69), calls=%async_computation | async-start | bytes 2097152 | tf_op jit(solution)/shard_map/while/body/eval_jaxpr/all_to_all | solution.py:112
  853.3 27.9 %all-to-all-start.1 = ((bf16[32,7,2048]{2,1,0:T(8,128)(2,1)}), bf16[32,7,2048]{2,1,0:T(8,128)(2,1)S(1)}, u32[]{:S(2)}, u32[]{:S(2)}) async-start(bf16[32,7,2048]{2,1,0:T(8,128)(2,1)} %reshape.63), calls=%async_computation.1 | async-start | bytes 2097152 | tf_op jit(solution)/shard_map/while/body/eval_jaxpr/all_to_all | solution.py:115
  882.6 13.8 %collective-permute-start = (bf16[32,2048]{1,0:T(8,128)(2,1)S(1)}, bf16[32,2048]{1,0:T(8,128)(2,1)S(1)}, u32[]{:S(2)}, u32[]{:S(2)}) collective-permute-start(bf16[32,2048]{1,0:T(8,128)(2,1)S(1)} %get-tuple-element.542), channel_id=1, source_target_pairs={{0,32},{32,64},{64,96},{96,128},{128,160},{160,192},{192,224},{1,3... | collective-permute-start | bytes 393224 | tf_op jit(solution)/shard_map/while/body/eval_jaxpr/ppermute | solution.py:20
where the time goes:
time: 920 us; the launch traced here: 916 us
  waiting for transfers between devices  563 us (61%)
  starting transfers between devices  180 us (20%)
  matrix products  63.6 us (7%)
  local copies, waits for them, and re-layouts  49.8 us (5%)
  blocking collectives  43.4 us (5%)
  other arithmetic  14.7 us (2%)
    all_to_all x11, waiting for transfers between devices, section_work(): received = lax.all_to_all(sent, DP, split_axis=0, concat_axis=0, tiled=True)  221 us
    all_to_all x11, waiting for transfers between devices, section_work(): lax.all_to_all(produced.reshape(received.shape), DP, split_axis=0, concat...  206 us
    ppermute x11, waiting for transfers between devices, from_behind(): lax.ppermute(value, axis, [(source, source + steps) for source in range(i...  136 us
    all_to_all x11, starting transfers between devices, section_work(): received = lax.all_to_all(sent, DP, split_axis=0, concat_axis=0, tiled=True)  82.5 us
    all_to_all x11, starting transfers between devices, section_work(): lax.all_to_all(produced.reshape(received.shape), DP, split_axis=0, concat...  76.3 us
    psum x2, blocking collectives, over_axes(): shard = lax.psum(shard, axis)  25 us
    ppermute x11, starting transfers between devices, from_behind(): lax.ppermute(value, axis, [(source, source + steps) for source in range(i...  21 us
    dot_general x4, matrix products, expert_ffn(): jnp.dot(hidden, w_down, preferred_element_type=jnp.float32)  19.9 us
  transfers between devices with their start and end apart: 33, of which 33 were waited for; matrix products, arithmetic and copies ran while one was open for 2% of the time, Pallas kernels for 0%

commit v1 on v0

--- a/solution.py
+++ b/solution.py
@@ -10,7 +10,7 @@
 
 def over_axes(shard, axes):
     for axis in axes:
-        shard = lax.psum(shard, axis)
+        shard = jnp.sum(jax.lax.all_gather(shard, axis_name=axis), axis=0)
     return shard
 
 

time: 920 us -> 924 us (level)
    psum x2 -> x0, blocking collectives: 25 us -> none  [over_axes(): shard = lax.psum(shard, axis)]
    unnamed x0 -> x2, blocking collectives: none -> 25 us
where the time goes in v1:
time: 924 us; the launch traced here: 921 us
  waiting for transfers between devices  563 us (61%)
  starting transfers between devices  180 us (19%)
  matrix products  63.5 us (7%)
  local copies, waits for them, and re-layouts  53 us (6%)
  blocking collectives  43.4 us (5%)
  other arithmetic  14.8 us (2%)
    all_to_all x11, waiting for transfers between devices, section_work(): received = lax.all_to_all(sent, DP, split_axis=0, concat_axis=0, tiled=True)  221 us
    all_to_all x11, waiting for transfers between devices, section_work(): lax.all_to_all(produced.reshape(received.shape), DP, split_axis=0, concat...  206 us
    ppermute x11, waiting for transfers between devices, from_behind(): lax.ppermute(value, axis, [(source, source + steps) for source in range(i...  136 us
    all_to_all x11, starting transfers between devices, section_work(): received = lax.all_to_all(sent, DP, split_axis=0, concat_axis=0, tiled=True)  82.5 us
    all_to_all x11, starting transfers between devices, section_work(): lax.all_to_all(produced.reshape(received.shape), DP, split_axis=0, concat...  76.1 us
    unnamed x2, blocking collectives  25 us
    ppermute x11, starting transfers between devices, from_behind(): lax.ppermute(value, axis, [(source, source + steps) for source in range(i...  21 us
    dot_general x4, matrix products, expert_ffn(): jnp.dot(hidden, w_down, preferred_element_type=jnp.float32)  19.9 us
  transfers between devices with their start and end apart: 33, of which 33 were waited for; matrix products, arithmetic and copies ran while one was open for 2% of the time, Pallas kernels for 0%

profile of v1, /device:TPU:8, one launch (start us, length us, event | category | flops | bytes accessed | tf_op | source)
XLA Modules:
  0.0 920.8 jit_solution(5920666272640544793)
XLA Ops:
  3.7 8.9 all-reduce
  14.9 16.1 %all-reduce.1 = s32[256]{0:T(256)S(1)} all-reduce(s32[256]{0:T(256)S(1)} %dynamic-update-slice.1), channel_id=3, replica_groups=mesh['section'=8,'dp_0'=4,'dp_1'=8] {'dp_1'}, use_global_device_ids=true, to_apply=%add.1 | all-reduce | flops 256 | bytes 2048
  33.9 867.1 %while.19 = (s32[]{:T(128)}, bf16[32,2048]{1,0:T(8,128)(2,1)S(1)}, bf16[4,32,2048]{2,1,0:T(8,128)(2,1)}, f32[2048,32]{0,1:T(8,128)S(1)}, pred[]{:T(512)}, /*inde...) while((s32[]{:T(128)}, bf16[32,2048]{1,0:T(8,128)(2,1)S(1)}, ...), condition=%wide.region_11.12_spmd.clone, body=%wide.region_4.11_spmd.clone.sunk | while | flops 2205590528 | bytes 29810108 | solution.py:150
  41.6 23.3 %all-to-all-done = bf16[32,7,2048]{2,1,0:T(8,128)(2,1)S(1)} async-done(((bf16[32,7,2048]{2,1,0:T(8,128)(2,1)}), bf16[32,7,2048]{2,1,0:T(8,128)(2,1)S(1)}, u32[]{:S(2)}, u32[]{:S(2)}) %all-to-all-start) | async-done | bytes 917536 | tf_op jit(solution)/shard_map/while/body/eval_jaxpr/all_to_all | solution.py:112
  73.3 21.5 %all-to-all-done.1 = bf16[32,7,2048]{2,1,0:T(8,128)(2,1)S(1)} async-done(((bf16[32,7,2048]{2,1,0:T(8,128)(2,1)}), bf16[32,7,2048]{2,1,0:T(8,128)(2,1)S(1)}, u32[]{:S(2)}, u32[]{:S(2)}) %all-to-all-start.1) | async-done | bytes 917536 | tf_op jit(solution)/shard_map/while/body/eval_jaxpr/all_to_all | solution.py:115
  111.6 28.2 %all-to-all-done = bf16[32,7,2048]{2,1,0:T(8,128)(2,1)S(1)} async-done(((bf16[32,7,2048]{2,1,0:T(8,128)(2,1)}), bf16[32,7,2048]{2,1,0:T(8,128)(2,1)S(1)}, u32[]{:S(2)}, u32[]{:S(2)}) %all-to-all-start) | async-done | bytes 917536 | tf_op jit(solution)/shard_map/while/body/eval_jaxpr/all_to_all | solution.py:112
  147.6 26.8 %all-to-all-done.1 = bf16[32,7,2048]{2,1,0:T(8,128)(2,1)S(1)} async-done(((bf16[32,7,2048]{2,1,0:T(8,128)(2,1)}), bf16[32,7,2048]{2,1,0:T(8,128)(2,1)S(1)}, u32[]{:S(2)}, u32[]{:S(2)}) %all-to-all-start.1) | async-done | bytes 917536 | tf_op jit(solution)/shard_map/while/body/eval_jaxpr/all_to_all | solution.py:115
  189.6 8.7 all-to-all-start
  198.3 20.5 %all-to-all-done = bf16[32,7,2048]{2,1,0:T(8,128)(2,1)S(1)} async-done(((bf16[32,7,2048]{2,1,0:T(8,128)(2,1)}), bf16[32,7,2048]{2,1,0:T(8,128)(2,1)S(1)}, u32[]{:S(2)}, u32[]{:S(2)}) %all-to-all-start) | async-done | bytes 917536 | tf_op jit(solution)/shard_map/while/body/eval_jaxpr/all_to_all | solution.py:112
  218.8 8.9 conditional.3
  234.8 16.7 %all-to-all-done.1 = bf16[32,7,2048]{2,1,0:T(8,128)(2,1)S(1)} async-done(((bf16[32,7,2048]{2,1,0:T(8,128)(2,1)}), bf16[32,7,2048]{2,1,0:T(8,128)(2,1)S(1)}, u32[]{:S(2)}, u32[]{:S(2)}) %all-to-all-start.1) | async-done | bytes 917536 | tf_op jit(solution)/shard_map/while/body/eval_jaxpr/all_to_all | solution.py:115
  255.1 17.5 %collective-permute-done = bf16[32,2048]{1,0:T(8,128)(2,1)S(1)} collective-permute-done((bf16[32,2048]{1,0:T(8,128)(2,1)S(1)}, bf16[32,2048]{1,0:T(8,128)(2,1)S(1)}, u32[]{:S(2)}, u32[]{:S(2)}) %collective-permute-start) | collective-permute-done | bytes 131104 | tf_op jit(solution)/shard_map/while/body/eval_jaxpr/ppermute | solution.py:20
  276.1 8.3 all-to-all-start
  284.4 18.1 %all-to-all-done = bf16[32,7,2048]{2,1,0:T(8,128)(2,1)S(1)} async-done(((bf16[32,7,2048]{2,1,0:T(8,128)(2,1)}), bf16[32,7,2048]{2,1,0:T(8,128)(2,1)S(1)}, u32[]{:S(2)}, u32[]{:S(2)}) %all-to-all-start) | async-done | bytes 917536 | tf_op jit(solution)/shard_map/while/body/eval_jaxpr/all_to_all | solution.py:112
  302.5 8.9 conditional.3
  320.4 16.7 %all-to-all-done.1 = bf16[32,7,2048]{2,1,0:T(8,128)(2,1)S(1)} async-done(((bf16[32,7,2048]{2,1,0:T(8,128)(2,1)}), bf16[32,7,2048]{2,1,0:T(8,128)(2,1)S(1)}, u32[]{:S(2)}, u32[]{:S(2)}) %all-to-all-start.1) | async-done | bytes 917536 | tf_op jit(solution)/shard_map/while/body/eval_jaxpr/all_to_all | solution.py:115
  340.7 18.0 %collective-permute-done = bf16[32,2048]{1,0:T(8,128)(2,1)S(1)} collective-permute-done((bf16[32,2048]{1,0:T(8,128)(2,1)S(1)}, bf16[32,2048]{1,0:T(8,128)(2,1)S(1)}, u32[]{:S(2)}, u32[]{:S(2)}) %collective-permute-start) | collective-permute-done | bytes 131104 | tf_op jit(solution)/shard_map/while/body/eval_jaxpr/ppermute | solution.py:20
  370.4 18.1 %all-to-all-done = bf16[32,7,2048]{2,1,0:T(8,128)(2,1)S(1)} async-done(((bf16[32,7,2048]{2,1,0:T(8,128)(2,1)}), bf16[32,7,2048]{2,1,0:T(8,128)(2,1)S(1)}, u32[]{:S(2)}, u32[]{:S(2)}) %all-to-all-start) | async-done | bytes 917536 | tf_op jit(solution)/shard_map/while/body/eval_jaxpr/all_to_all | solution.py:112
  388.5 8.9 conditional.3
  406.5 16.7 %all-to-all-done.1 = bf16[32,7,2048]{2,1,0:T(8,128)(2,1)S(1)} async-done(((bf16[32,7,2048]{2,1,0:T(8,128)(2,1)}), bf16[32,7,2048]{2,1,0:T(8,128)(2,1)S(1)}, u32[]{:S(2)}, u32[]{:S(2)}) %all-to-all-start.1) | async-done | bytes 917536 | tf_op jit(solution)/shard_map/while/body/eval_jaxpr/all_to_all | solution.py:115
  426.8 13.2 %collective-permute-done = bf16[32,2048]{1,0:T(8,128)(2,1)S(1)} collective-permute-done((bf16[32,2048]{1,0:T(8,128)(2,1)S(1)}, bf16[32,2048]{1,0:T(8,128)(2,1)S(1)}, u32[]{:S(2)}, u32[]{:S(2)}) %collective-permute-start) | collective-permute-done | bytes 131104 | tf_op jit(solution)/shard_map/while/body/eval_jaxpr/ppermute | solution.py:20
  449.3 17.5 %all-to-all-done = bf16[32,7,2048]{2,1,0:T(8,128)(2,1)S(1)} async-done(((bf16[32,7,2048]{2,1,0:T(8,128)(2,1)}), bf16[32,7,2048]{2,1,0:T(8,128)(2,1)S(1)}, u32[]{:S(2)}, u32[]{:S(2)}) %all-to-all-start) | async-done | bytes 917536 | tf_op jit(solution)/shard_map/while/body/eval_jaxpr/all_to_all | solution.py:112
  466.8 8.9 conditional.3
  484.9 16.7 %all-to-all-done.1 = bf16[32,7,2048]{2,1,0:T(8,128)(2,1)S(1)} async-done(((bf16[32,7,2048]{2,1,0:T(8,128)(2,1)}), bf16[32,7,2048]{2,1,0:T(8,128)(2,1)S(1)}, u32[]{:S(2)}, u32[]{:S(2)}) %all-to-all-start.1) | async-done | bytes 917536 | tf_op jit(solution)/shard_map/while/body/eval_jaxpr/all_to_all | solution.py:115
  505.2 9.6 %collective-permute-done = bf16[32,2048]{1,0:T(8,128)(2,1)S(1)} collective-permute-done((bf16[32,2048]{1,0:T(8,128)(2,1)S(1)}, bf16[32,2048]{1,0:T(8,128)(2,1)S(1)}, u32[]{:S(2)}, u32[]{:S(2)}) %collective-permute-start) | collective-permute-done | bytes 131104 | tf_op jit(solution)/shard_map/while/body/eval_jaxpr/ppermute | solution.py:20
  526.6 17.8 %all-to-all-done = bf16[32,7,2048]{2,1,0:T(8,128)(2,1)S(1)} async-done(((bf16[32,7,2048]{2,1,0:T(8,128)(2,1)}), bf16[32,7,2048]{2,1,0:T(8,128)(2,1)S(1)}, u32[]{:S(2)}, u32[]{:S(2)}) %all-to-all-start) | async-done | bytes 917536 | tf_op jit(solution)/shard_map/while/body/eval_jaxpr/all_to_all | solution.py:112
  553.3 24.1 %all-to-all-done.1 = bf16[32,7,2048]{2,1,0:T(8,128)(2,1)S(1)} async-done(((bf16[32,7,2048]{2,1,0:T(8,128)(2,1)}), bf16[32,7,2048]{2,1,0:T(8,128)(2,1)S(1)}, u32[]{:S(2)}, u32[]{:S(2)}) %all-to-all-start.1) | async-done | bytes 917536 | tf_op jit(solution)/shard_map/while/body/eval_jaxpr/all_to_all | solution.py:115
  581.1 11.0 %collective-permute-done = bf16[32,2048]{1,0:T(8,128)(2,1)S(1)} collective-permute-done((bf16[32,2048]{1,0:T(8,128)(2,1)S(1)}, bf16[32,2048]{1,0:T(8,128)(2,1)S(1)}, u32[]{:S(2)}, u32[]{:S(2)}) %collective-permute-start) | collective-permute-done | bytes 131104 | tf_op jit(solution)/shard_map/while/body/eval_jaxpr/ppermute | solution.py:20
  595.5 8.3 all-to-all-start
  603.8 18.1 %all-to-all-done = bf16[32,7,2048]{2,1,0:T(8,128)(2,1)S(1)} async-done(((bf16[32,7,2048]{2,1,0:T(8,128)(2,1)}), bf16[32,7,2048]{2,1,0:T(8,128)(2,1)S(1)}, u32[]{:S(2)}, u32[]{:S(2)}) %all-to-all-start) | async-done | bytes 917536 | tf_op jit(solution)/shard_map/while/body/eval_jaxpr/all_to_all | solution.py:112
  623.3 8.4 all-to-all-start.1
  633.1 16.7 %all-to-all-done.1 = bf16[32,7,2048]{2,1,0:T(8,128)(2,1)S(1)} async-done(((bf16[32,7,2048]{2,1,0:T(8,128)(2,1)}), bf16[32,7,2048]{2,1,0:T(8,128)(2,1)S(1)}, u32[]{:S(2)}, u32[]{:S(2)}) %all-to-all-start.1) | async-done | bytes 917536 | tf_op jit(solution)/shard_map/while/body/eval_jaxpr/all_to_all | solution.py:115
  653.4 15.8 %collective-permute-done = bf16[32,2048]{1,0:T(8,128)(2,1)S(1)} collective-permute-done((bf16[32,2048]{1,0:T(8,128)(2,1)S(1)}, bf16[32,2048]{1,0:T(8,128)(2,1)S(1)}, u32[]{:S(2)}, u32[]{:S(2)}) %collective-permute-start) | collective-permute-done | bytes 131104 | tf_op jit(solution)/shard_map/while/body/eval_jaxpr/ppermute | solution.py:20
  672.7 8.3 all-to-all-start
  681.0 20.6 %all-to-all-done = bf16[32,7,2048]{2,1,0:T(8,128)(2,1)S(1)} async-done(((bf16[32,7,2048]{2,1,0:T(8,128)(2,1)}), bf16[32,7,2048]{2,1,0:T(8,128)(2,1)S(1)}, u32[]{:S(2)}, u32[]{:S(2)}) %all-to-all-start) | async-done | bytes 917536 | tf_op jit(solution)/shard_map/while/body/eval_jaxpr/all_to_all | solution.py:112
  703.0 10.2 %all-to-all-start.1 = ((bf16[32,7,2048]{2,1,0:T(8,128)(2,1)}), bf16[32,7,2048]{2,1,0:T(8,128)(2,1)S(1)}, u32[]{:S(2)}, u32[]{:S(2)}) async-start(bf16[32,7,2048]{2,1,0:T(8,128)(2,1)} %reshape.75), calls=%async_computation.1 | async-start | bytes 2097152 | tf_op jit(solution)/shard_map/while/body/eval_jaxpr/all_to_all | solution.py:115
  714.6 16.7 %all-to-all-done.1 = bf16[32,7,2048]{2,1,0:T(8,128)(2,1)S(1)} async-done(((bf16[32,7,2048]{2,1,0:T(8,128)(2,1)}), bf16[32,7,2048]{2,1,0:T(8,128)(2,1)S(1)}, u32[]{:S(2)}, u32[]{:S(2)}) %all-to-all-start.1) | async-done | bytes 917536 | tf_op jit(solution)/shard_map/while/body/eval_jaxpr/all_to_all | solution.py:115
  734.9 11.5 %collective-permute-done = bf16[32,2048]{1,0:T(8,128)(2,1)S(1)} collective-permute-done((bf16[32,2048]{1,0:T(8,128)(2,1)S(1)}, bf16[32,2048]{1,0:T(8,128)(2,1)S(1)}, u32[]{:S(2)}, u32[]{:S(2)}) %collective-permute-start) | collective-permute-done | bytes 131104 | tf_op jit(solution)/shard_map/while/body/eval_jaxpr/ppermute | solution.py:20
  750.0 8.3 all-to-all-start
  758.3 18.1 %all-to-all-done = bf16[32,7,2048]{2,1,0:T(8,128)(2,1)S(1)} async-done(((bf16[32,7,2048]{2,1,0:T(8,128)(2,1)}), bf16[32,7,2048]{2,1,0:T(8,128)(2,1)S(1)}, u32[]{:S(2)}, u32[]{:S(2)}) %all-to-all-start) | async-done | bytes 917536 | tf_op jit(solution)/shard_map/while/body/eval_jaxpr/all_to_all | solution.py:112
  787.4 16.7 %all-to-all-done.1 = bf16[32,7,2048]{2,1,0:T(8,128)(2,1)S(1)} async-done(((bf16[32,7,2048]{2,1,0:T(8,128)(2,1)}), bf16[32,7,2048]{2,1,0:T(8,128)(2,1)S(1)}, u32[]{:S(2)}, u32[]{:S(2)}) %all-to-all-start.1) | async-done | bytes 917536 | tf_op jit(solution)/shard_map/while/body/eval_jaxpr/all_to_all | solution.py:115
  807.7 16.0 %collective-permute-done = bf16[32,2048]{1,0:T(8,128)(2,1)S(1)} collective-permute-done((bf16[32,2048]{1,0:T(8,128)(2,1)S(1)}, bf16[32,2048]{1,0:T(8,128)(2,1)S(1)}, u32[]{:S(2)}, u32[]{:S(2)}) %collective-permute-start) | collective-permute-done | bytes 131104 | tf_op jit(solution)/shard_map/while/body/eval_jaxpr/ppermute | solution.py:20
  827.2 8.3 all-to-all-start
  835.5 20.9 %all-to-all-done = bf16[32,7,2048]{2,1,0:T(8,128)(2,1)S(1)} async-done(((bf16[32,7,2048]{2,1,0:T(8,128)(2,1)}), bf16[32,7,2048]{2,1,0:T(8,128)(2,1)S(1)}, u32[]{:S(2)}, u32[]{:S(2)}) %all-to-all-start) | async-done | bytes 917536 | tf_op jit(solution)/shard_map/while/body/eval_jaxpr/all_to_all | solution.py:112
  857.8 9.8 %all-to-all-start.1 = ((bf16[32,7,2048]{2,1,0:T(8,128)(2,1)}), bf16[32,7,2048]{2,1,0:T(8,128)(2,1)S(1)}, u32[]{:S(2)}, u32[]{:S(2)}) async-start(bf16[32,7,2048]{2,1,0:T(8,128)(2,1)} %reshape.75), calls=%async_computation.1 | async-start | bytes 2097152 | tf_op jit(solution)/shard_map/while/body/eval_jaxpr/all_to_all | solution.py:115
  869.1 16.7 %all-to-all-done.1 = bf16[32,7,2048]{2,1,0:T(8,128)(2,1)S(1)} async-done(((bf16[32,7,2048]{2,1,0:T(8,128)(2,1)}), bf16[32,7,2048]{2,1,0:T(8,128)(2,1)S(1)}, u32[]{:S(2)}, u32[]{:S(2)}) %all-to-all-start.1) | async-done | bytes 917536 | tf_op jit(solution)/shard_map/while/body/eval_jaxpr/all_to_all | solution.py:115
  889.4 11.6 %collective-permute-done = bf16[32,2048]{1,0:T(8,128)(2,1)S(1)} collective-permute-done((bf16[32,2048]{1,0:T(8,128)(2,1)S(1)}, bf16[32,2048]{1,0:T(8,128)(2,1)S(1)}, u32[]{:S(2)}, u32[]{:S(2)}) %collective-permute-start) | collective-permute-done | bytes 131104 | tf_op jit(solution)/shard_map/while/body/eval_jaxpr/ppermute | solution.py:20
  901.5 18.4 %all_to_all.29 = bf16[32,2,1024]{2,1,0:T(2,128)(2,1)S(1)} all-to-all(bf16[32,2,1024]{2,1,0:T(2,128)(2,1)S(1)} %reshape.72), channel_id=1, replica_groups=mesh['section'=8,'dp_0'=4,'dp_1'=8] {'dp_0','dp_1'}, dimensions={0} | all-to-all | bytes 262144 | tf_op jit(solution)/shard_map/all_to_all | solution.py:31
  (285 shorter events, 245.2 us)
Async XLA Ops:
  37.4 27.5 %all-to-all-start = ((bf16[32,7,2048]{2,1,0:T(8,128)(2,1)}), bf16[32,7,2048]{2,1,0:T(8,128)(2,1)S(1)}, u32[]{:S(2)}, u32[]{:S(2)}) async-start(bf16[32,7,2048]{2,1,0:T(8,128)(2,1)} %copy.69), calls=%async_computation | async-start | bytes 2097152 | tf_op jit(solution)/shard_map/while/body/eval_jaxpr/all_to_all | solution.py:112
  66.3 28.5 %all-to-all-start.1 = ((bf16[32,7,2048]{2,1,0:T(8,128)(2,1)}), bf16[32,7,2048]{2,1,0:T(8,128)(2,1)S(1)}, u32[]{:S(2)}, u32[]{:S(2)}) async-start(bf16[32,7,2048]{2,1,0:T(8,128)(2,1)} %reshape.75), calls=%async_computation.1 | async-start | bytes 2097152 | tf_op jit(solution)/shard_map/while/body/eval_jaxpr/all_to_all | solution.py:115
  96.1 6.3 collective-permute-start
  105.9 33.9 %all-to-all-start = ((bf16[32,7,2048]{2,1,0:T(8,128)(2,1)}), bf16[32,7,2048]{2,1,0:T(8,128)(2,1)S(1)}, u32[]{:S(2)}, u32[]{:S(2)}) async-start(bf16[32,7,2048]{2,1,0:T(8,128)(2,1)} %copy.69), calls=%async_computation | async-start | bytes 2097152 | tf_op jit(solution)/shard_map/while/body/eval_jaxpr/all_to_all | solution.py:112
  141.2 33.2 %all-to-all-start.1 = ((bf16[32,7,2048]{2,1,0:T(8,128)(2,1)}), bf16[32,7,2048]{2,1,0:T(8,128)(2,1)S(1)}, u32[]{:S(2)}, u32[]{:S(2)}) async-start(bf16[32,7,2048]{2,1,0:T(8,128)(2,1)} %reshape.75), calls=%async_computation.1 | async-start | bytes 2097152 | tf_op jit(solution)/shard_map/while/body/eval_jaxpr/all_to_all | solution.py:115
  175.8 10.3 %collective-permute-start = (bf16[32,2048]{1,0:T(8,128)(2,1)S(1)}, bf16[32,2048]{1,0:T(8,128)(2,1)S(1)}, u32[]{:S(2)}, u32[]{:S(2)}) collective-permute-start(bf16[32,2048]{1,0:T(8,128)(2,1)S(1)} %get-tuple-element.542), channel_id=1, source_target_pairs={{0,32},{32,64},{64,96},{96,128},{128,160},{160,192},{192,224},{1,3... | collective-permute-start | bytes 393224 | tf_op jit(solution)/shard_map/while/body/eval_jaxpr/ppermute | solution.py:20
  189.6 29.2 %all-to-all-start = ((bf16[32,7,2048]{2,1,0:T(8,128)(2,1)}), bf16[32,7,2048]{2,1,0:T(8,128)(2,1)S(1)}, u32[]{:S(2)}, u32[]{:S(2)}) async-start(bf16[32,7,2048]{2,1,0:T(8,128)(2,1)} %copy.69), calls=%async_computation | async-start | bytes 2097152 | tf_op jit(solution)/shard_map/while/body/eval_jaxpr/all_to_all | solution.py:112
  229.0 22.4 %all-to-all-start.1 = ((bf16[32,7,2048]{2,1,0:T(8,128)(2,1)}), bf16[32,7,2048]{2,1,0:T(8,128)(2,1)S(1)}, u32[]{:S(2)}, u32[]{:S(2)}) async-start(bf16[32,7,2048]{2,1,0:T(8,128)(2,1)} %reshape.75), calls=%async_computation.1 | async-start | bytes 2097152 | tf_op jit(solution)/shard_map/while/body/eval_jaxpr/all_to_all | solution.py:115
  252.8 19.8 %collective-permute-start = (bf16[32,2048]{1,0:T(8,128)(2,1)S(1)}, bf16[32,2048]{1,0:T(8,128)(2,1)S(1)}, u32[]{:S(2)}, u32[]{:S(2)}) collective-permute-start(bf16[32,2048]{1,0:T(8,128)(2,1)S(1)} %get-tuple-element.542), channel_id=1, source_target_pairs={{0,32},{32,64},{64,96},{96,128},{128,160},{160,192},{192,224},{1,3... | collective-permute-start | bytes 393224 | tf_op jit(solution)/shard_map/while/body/eval_jaxpr/ppermute | solution.py:20
  276.1 26.4 %all-to-all-start = ((bf16[32,7,2048]{2,1,0:T(8,128)(2,1)}), bf16[32,7,2048]{2,1,0:T(8,128)(2,1)S(1)}, u32[]{:S(2)}, u32[]{:S(2)}) async-start(bf16[32,7,2048]{2,1,0:T(8,128)(2,1)} %copy.69), calls=%async_computation | async-start | bytes 2097152 | tf_op jit(solution)/shard_map/while/body/eval_jaxpr/all_to_all | solution.py:112
  312.7 24.4 %all-to-all-start.1 = ((bf16[32,7,2048]{2,1,0:T(8,128)(2,1)}), bf16[32,7,2048]{2,1,0:T(8,128)(2,1)S(1)}, u32[]{:S(2)}, u32[]{:S(2)}) async-start(bf16[32,7,2048]{2,1,0:T(8,128)(2,1)} %reshape.75), calls=%async_computation.1 | async-start | bytes 2097152 | tf_op jit(solution)/shard_map/while/body/eval_jaxpr/all_to_all | solution.py:115
  338.4 20.2 %collective-permute-start = (bf16[32,2048]{1,0:T(8,128)(2,1)S(1)}, bf16[32,2048]{1,0:T(8,128)(2,1)S(1)}, u32[]{:S(2)}, u32[]{:S(2)}) collective-permute-start(bf16[32,2048]{1,0:T(8,128)(2,1)S(1)} %get-tuple-element.542), channel_id=1, source_target_pairs={{0,32},{32,64},{64,96},{96,128},{128,160},{160,192},{192,224},{1,3... | collective-permute-start | bytes 393224 | tf_op jit(solution)/shard_map/while/body/eval_jaxpr/ppermute | solution.py:20
  362.1 26.4 %all-to-all-start = ((bf16[32,7,2048]{2,1,0:T(8,128)(2,1)}), bf16[32,7,2048]{2,1,0:T(8,128)(2,1)S(1)}, u32[]{:S(2)}, u32[]{:S(2)}) async-start(bf16[32,7,2048]{2,1,0:T(8,128)(2,1)} %copy.69), calls=%async_computation | async-start | bytes 2097152 | tf_op jit(solution)/shard_map/while/body/eval_jaxpr/all_to_all | solution.py:112
  398.8 24.4 %all-to-all-start.1 = ((bf16[32,7,2048]{2,1,0:T(8,128)(2,1)}), bf16[32,7,2048]{2,1,0:T(8,128)(2,1)S(1)}, u32[]{:S(2)}, u32[]{:S(2)}) async-start(bf16[32,7,2048]{2,1,0:T(8,128)(2,1)} %reshape.75), calls=%async_computation.1 | async-start | bytes 2097152 | tf_op jit(solution)/shard_map/while/body/eval_jaxpr/all_to_all | solution.py:115
  424.5 15.4 %collective-permute-start = (bf16[32,2048]{1,0:T(8,128)(2,1)S(1)}, bf16[32,2048]{1,0:T(8,128)(2,1)S(1)}, u32[]{:S(2)}, u32[]{:S(2)}) collective-permute-start(bf16[32,2048]{1,0:T(8,128)(2,1)S(1)} %get-tuple-element.542), channel_id=1, source_target_pairs={{0,32},{32,64},{64,96},{96,128},{128,160},{160,192},{192,224},{1,3... | collective-permute-start | bytes 393224 | tf_op jit(solution)/shard_map/while/body/eval_jaxpr/ppermute | solution.py:20
  443.4 23.4 %all-to-all-start = ((bf16[32,7,2048]{2,1,0:T(8,128)(2,1)}), bf16[32,7,2048]{2,1,0:T(8,128)(2,1)S(1)}, u32[]{:S(2)}, u32[]{:S(2)}) async-start(bf16[32,7,2048]{2,1,0:T(8,128)(2,1)} %copy.69), calls=%async_computation | async-start | bytes 2097152 | tf_op jit(solution)/shard_map/while/body/eval_jaxpr/all_to_all | solution.py:112
  477.0 24.5 %all-to-all-start.1 = ((bf16[32,7,2048]{2,1,0:T(8,128)(2,1)}), bf16[32,7,2048]{2,1,0:T(8,128)(2,1)S(1)}, u32[]{:S(2)}, u32[]{:S(2)}) async-start(bf16[32,7,2048]{2,1,0:T(8,128)(2,1)} %reshape.75), calls=%async_computation.1 | async-start | bytes 2097152 | tf_op jit(solution)/shard_map/while/body/eval_jaxpr/all_to_all | solution.py:115
  503.0 11.9 %collective-permute-start = (bf16[32,2048]{1,0:T(8,128)(2,1)S(1)}, bf16[32,2048]{1,0:T(8,128)(2,1)S(1)}, u32[]{:S(2)}, u32[]{:S(2)}) collective-permute-start(bf16[32,2048]{1,0:T(8,128)(2,1)S(1)} %get-tuple-element.542), channel_id=1, source_target_pairs={{0,32},{32,64},{64,96},{96,128},{128,160},{160,192},{192,224},{1,3... | collective-permute-start | bytes 393224 | tf_op jit(solution)/shard_map/while/body/eval_jaxpr/ppermute | solution.py:20
  518.3 26.1 %all-to-all-start = ((bf16[32,7,2048]{2,1,0:T(8,128)(2,1)}), bf16[32,7,2048]{2,1,0:T(8,128)(2,1)S(1)}, u32[]{:S(2)}, u32[]{:S(2)}) async-start(bf16[32,7,2048]{2,1,0:T(8,128)(2,1)} %copy.69), calls=%async_computation | async-start | bytes 2097152 | tf_op jit(solution)/shard_map/while/body/eval_jaxpr/all_to_all | solution.py:112
  545.8 31.7 %all-to-all-start.1 = ((bf16[32,7,2048]{2,1,0:T(8,128)(2,1)}), bf16[32,7,2048]{2,1,0:T(8,128)(2,1)S(1)}, u32[]{:S(2)}, u32[]{:S(2)}) async-start(bf16[32,7,2048]{2,1,0:T(8,128)(2,1)} %reshape.75), calls=%async_computation.1 | async-start | bytes 2097152 | tf_op jit(solution)/shard_map/while/body/eval_jaxpr/all_to_all | solution.py:115
  578.8 13.2 %collective-permute-start = (bf16[32,2048]{1,0:T(8,128)(2,1)S(1)}, bf16[32,2048]{1,0:T(8,128)(2,1)S(1)}, u32[]{:S(2)}, u32[]{:S(2)}) collective-permute-start(bf16[32,2048]{1,0:T(8,128)(2,1)S(1)} %get-tuple-element.542), channel_id=1, source_target_pairs={{0,32},{32,64},{64,96},{96,128},{128,160},{160,192},{192,224},{1,3... | collective-permute-start | bytes 393224 | tf_op jit(solution)/shard_map/while/body/eval_jaxpr/ppermute | solution.py:20
  595.5 26.4 %all-to-all-start = ((bf16[32,7,2048]{2,1,0:T(8,128)(2,1)}), bf16[32,7,2048]{2,1,0:T(8,128)(2,1)S(1)}, u32[]{:S(2)}, u32[]{:S(2)}) async-start(bf16[32,7,2048]{2,1,0:T(8,128)(2,1)} %copy.69), calls=%async_computation | async-start | bytes 2097152 | tf_op jit(solution)/shard_map/while/body/eval_jaxpr/all_to_all | solution.py:112
  623.3 26.5 %all-to-all-start.1 = ((bf16[32,7,2048]{2,1,0:T(8,128)(2,1)}), bf16[32,7,2048]{2,1,0:T(8,128)(2,1)S(1)}, u32[]{:S(2)}, u32[]{:S(2)}) async-start(bf16[32,7,2048]{2,1,0:T(8,128)(2,1)} %reshape.75), calls=%async_computation.1 | async-start | bytes 2097152 | tf_op jit(solution)/shard_map/while/body/eval_jaxpr/all_to_all | solution.py:115
  651.2 18.1 %collective-permute-start = (bf16[32,2048]{1,0:T(8,128)(2,1)S(1)}, bf16[32,2048]{1,0:T(8,128)(2,1)S(1)}, u32[]{:S(2)}, u32[]{:S(2)}) collective-permute-start(bf16[32,2048]{1,0:T(8,128)(2,1)S(1)} %get-tuple-element.542), channel_id=1, source_target_pairs={{0,32},{32,64},{64,96},{96,128},{128,160},{160,192},{192,224},{1,3... | collective-permute-start | bytes 393224 | tf_op jit(solution)/shard_map/while/body/eval_jaxpr/ppermute | solution.py:20
  672.7 28.9 %all-to-all-start = ((bf16[32,7,2048]{2,1,0:T(8,128)(2,1)}), bf16[32,7,2048]{2,1,0:T(8,128)(2,1)S(1)}, u32[]{:S(2)}, u32[]{:S(2)}) async-start(bf16[32,7,2048]{2,1,0:T(8,128)(2,1)} %copy.69), calls=%async_computation | async-start | bytes 2097152 | tf_op jit(solution)/shard_map/while/body/eval_jaxpr/all_to_all | solution.py:112
  703.0 28.3 %all-to-all-start.1 = ((bf16[32,7,2048]{2,1,0:T(8,128)(2,1)}), bf16[32,7,2048]{2,1,0:T(8,128)(2,1)S(1)}, u32[]{:S(2)}, u32[]{:S(2)}) async-start(bf16[32,7,2048]{2,1,0:T(8,128)(2,1)} %reshape.75), calls=%async_computation.1 | async-start | bytes 2097152 | tf_op jit(solution)/shard_map/while/body/eval_jaxpr/all_to_all | solution.py:115
  732.7 13.8 %collective-permute-start = (bf16[32,2048]{1,0:T(8,128)(2,1)S(1)}, bf16[32,2048]{1,0:T(8,128)(2,1)S(1)}, u32[]{:S(2)}, u32[]{:S(2)}) collective-permute-start(bf16[32,2048]{1,0:T(8,128)(2,1)S(1)} %get-tuple-element.542), channel_id=1, source_target_pairs={{0,32},{32,64},{64,96},{96,128},{128,160},{160,192},{192,224},{1,3... | collective-permute-start | bytes 393224 | tf_op jit(solution)/shard_map/while/body/eval_jaxpr/ppermute | solution.py:20
  750.0 26.4 %all-to-all-start = ((bf16[32,7,2048]{2,1,0:T(8,128)(2,1)}), bf16[32,7,2048]{2,1,0:T(8,128)(2,1)S(1)}, u32[]{:S(2)}, u32[]{:S(2)}) async-start(bf16[32,7,2048]{2,1,0:T(8,128)(2,1)} %copy.69), calls=%async_computation | async-start | bytes 2097152 | tf_op jit(solution)/shard_map/while/body/eval_jaxpr/all_to_all | solution.py:112
  777.8 26.3 %all-to-all-start.1 = ((bf16[32,7,2048]{2,1,0:T(8,128)(2,1)}), bf16[32,7,2048]{2,1,0:T(8,128)(2,1)S(1)}, u32[]{:S(2)}, u32[]{:S(2)}) async-start(bf16[32,7,2048]{2,1,0:T(8,128)(2,1)} %reshape.75), calls=%async_computation.1 | async-start | bytes 2097152 | tf_op jit(solution)/shard_map/while/body/eval_jaxpr/all_to_all | solution.py:115
  805.5 18.3 %collective-permute-start = (bf16[32,2048]{1,0:T(8,128)(2,1)S(1)}, bf16[32,2048]{1,0:T(8,128)(2,1)S(1)}, u32[]{:S(2)}, u32[]{:S(2)}) collective-permute-start(bf16[32,2048]{1,0:T(8,128)(2,1)S(1)} %get-tuple-element.542), channel_id=1, source_target_pairs={{0,32},{32,64},{64,96},{96,128},{128,160},{160,192},{192,224},{1,3... | collective-permute-start | bytes 393224 | tf_op jit(solution)/shard_map/while/body/eval_jaxpr/ppermute | solution.py:20
  827.2 29.2 %all-to-all-start = ((bf16[32,7,2048]{2,1,0:T(8,128)(2,1)}), bf16[32,7,2048]{2,1,0:T(8,128)(2,1)S(1)}, u32[]{:S(2)}, u32[]{:S(2)}) async-start(bf16[32,7,2048]{2,1,0:T(8,128)(2,1)} %copy.69), calls=%async_computation | async-start | bytes 2097152 | tf_op jit(solution)/shard_map/while/body/eval_jaxpr/all_to_all | solution.py:112
  857.8 27.9 %all-to-all-start.1 = ((bf16[32,7,2048]{2,1,0:T(8,128)(2,1)}), bf16[32,7,2048]{2,1,0:T(8,128)(2,1)S(1)}, u32[]{:S(2)}, u32[]{:S(2)}) async-start(bf16[32,7,2048]{2,1,0:T(8,128)(2,1)} %reshape.75), calls=%async_computation.1 | async-start | bytes 2097152 | tf_op jit(solution)/shard_map/while/body/eval_jaxpr/all_to_all | solution.py:115
  887.1 13.8 %collective-permute-start = (bf16[32,2048]{1,0:T(8,128)(2,1)S(1)}, bf16[32,2048]{1,0:T(8,128)(2,1)S(1)}, u32[]{:S(2)}, u32[]{:S(2)}) collective-permute-start(bf16[32,2048]{1,0:T(8,128)(2,1)S(1)} %get-tuple-element.542), channel_id=1, source_target_pairs={{0,32},{32,64},{64,96},{96,128},{128,160},{160,192},{192,224},{1,3... | collective-permute-start | bytes 393224 | tf_op jit(solution)/shard_map/while/body/eval_jaxpr/ppermute | solution.py:20
